TPU v7x, 32 devices: a whole 2x2x4 slice. The times are simulated.
32 devices in a mesh: depth: 4 (over z), row: 2 (over core), col: 4 (over y, x).
Axes of the slice: x: 2, y: 2, z: 4, core: 2. Of those that a mesh axis runs over, the one named last changes fastest.
Arguments:
- volume: bfloat16 [4, 18, 256, 8192], P('depth', None, 'row', 'col'), may hold values from -6 to 6
- order: int32 [4], replicated, may hold values from 0 to 3, each once
- empty: int32 [4, 2, 4], P('depth', 'row', 'col'), may hold values 0 or 1
- bump_center: float32 [4], replicated, may hold values from -1.5 to 1.5
- bump_width: float32 [4], replicated, may hold values from 0.3 to 1
- bump_height: float32 [4], replicated, may hold values from 0.5 to 4
- bump_color: float32 [3, 4], replicated, may hold values from 0.5 to 2
- light_dir: float32 [3], replicated, may hold values from -1 to 1
Outputs:
- image: float32 [2, 4, 128, 8192], P('row', None, 'depth', 'col')
Inputs may be any that keep to these rules, and one draw needn't show every extreme that they name: `order`: a permutation of the depth indices.
All inputs are finite; a program needn't handle non-finite values. No bound on the sum of `empty` on one device may be relied on, other than what follows from the above.
Results may differ from a plain program's by a relative error of at most 0.0003.
Values may be sent and summed in bfloat16 or wider, within the bound.
No kernel may reach another device: no remote copies, remote signals or barrier semaphores. Data moves between devices by JAX's collectives and lax.ppermute only.
A program may use at most 128 MiB of HBM per device.

v0:
```python
import jax
import jax.numpy as jnp
from jax import lax
from jax.sharding import PartitionSpec as P

slab_depth = 8
absorption = 0.08


def with_halo(x, sides, width):
    for axis, dim in sides:
        count, length = (lax.axis_size(axis), x.shape[dim])
        up = [(i, (i + 1) % count) for i in range(count - 1)]
        down = [(j, i) for i, j in up]
        last = lax.slice_in_dim(x, length - width, length, axis=dim)
        leading = lax.slice_in_dim(x, 0, width, axis=dim)
        before = lax.ppermute(last, axis, up)
        after = lax.ppermute(leading, axis, down)
        x = jnp.concatenate([before, x, after], axis=dim)
    return x


def march_brick(padded, bump_center, bump_width, bump_height, bump_color, light_dir):
    depth_len = padded.shape[0] - 2
    row_count = padded.shape[1] - 2
    col_count = padded.shape[2] - 2
    per_sample = absorption / depth_len

    def advance(state_pair, slab_index):
        through, radiance = state_pair
        block_cells = lax.dynamic_slice_in_dim(
            padded, slab_index * slab_depth, slab_depth + 2, 0
        ).astype(jnp.float32)
        samples = block_cells[1:-1, 1:-1, 1:-1]
        grad_z = 0.5 * (block_cells[2:, 1:-1, 1:-1] - block_cells[:-2, 1:-1, 1:-1])
        grad_y = 0.5 * (block_cells[1:-1, 2:, 1:-1] - block_cells[1:-1, :-2, 1:-1])
        grad_x = 0.5 * (block_cells[1:-1, 1:-1, 2:] - block_cells[1:-1, 1:-1, :-2])
        facing = jnp.abs(light_dir[0] * grad_z + light_dir[1] * grad_y + light_dir[2] * grad_x)
        shading = 0.3 + 0.7 * facing / jnp.sqrt(
            grad_z * grad_z + grad_y * grad_y + grad_x * grad_x + 1.0
        )
        density = jnp.zeros_like(samples)
        emission = [jnp.zeros_like(samples) for channel in range(3)]
        for bump_index in range(bump_center.shape[0]):
            offset = samples - bump_center[bump_index]
            bump_value = jnp.exp(
                -offset * offset / (2.0 * bump_width[bump_index] * bump_width[bump_index])
            )
            density = density + bump_height[bump_index] * bump_value
            emission = [
                emission[channel] + bump_color[channel, bump_index] * bump_value
                for channel in range(3)
            ]
        passing = jnp.exp(-per_sample * density)
        inclusive = jnp.cumprod(passing, axis=0)
        transmit = jnp.concatenate([jnp.ones_like(passing[:1]), inclusive[:-1]], 0) * through
        weights = transmit * (1.0 - passing) * shading
        radiance = radiance + jnp.stack(
            [jnp.sum(weights * emission[channel], 0) for channel in range(3)]
        )
        return ((through * inclusive[-1], radiance), None)

    start_carry = (
        jnp.ones((row_count, col_count), jnp.float32),
        jnp.zeros((3, row_count, col_count), jnp.float32),
    )
    (through, radiance), unused = lax.scan(
        advance, start_carry, jnp.arange(depth_len // slab_depth, dtype=jnp.int32)
    )
    return jnp.concatenate([radiance, (1.0 - through)[None]], 0)


def composite(stacked, order):
    ranked = jnp.take(stacked, order, axis=0)

    def layer_over(state_pair, layer_image):
        through, summed = state_pair
        summed = summed + through[None] * layer_image
        return ((through * (1.0 - layer_image[3]), summed), None)

    start_carry = (
        jnp.ones(stacked.shape[2:], jnp.float32),
        jnp.zeros(stacked.shape[1:], jnp.float32),
    )
    (through, summed), unused = lax.scan(layer_over, start_carry, ranked)
    return summed


def per_device(volume, order, empty, bump_center, bump_width, bump_height, bump_color, light_dir):
    padded = with_halo(volume[0], (("row", 1), ("col", 2)), 1)
    row_count = volume.shape[2]
    col_count = volume.shape[3]

    def blank_layer():
        return jnp.zeros((4, row_count, col_count), jnp.float32)

    def lit_layer():
        return march_brick(padded, bump_center, bump_width, bump_height, bump_color, light_dir)

    layer_image = lax.cond(empty[0, 0, 0] == 1, blank_layer, lit_layer)
    band_rows = composite(
        lax.all_to_all(layer_image[None], "depth", split_axis=2, concat_axis=0, tiled=True), order
    )
    return band_rows[None]


def solution(mesh):
    placed = (
        P("depth", None, "row", "col"),
        P(),
        P("depth", "row", "col"),
        P(),
        P(),
        P(),
        P(),
        P(),
    )
    return jax.shard_map(
        per_device,
        mesh=mesh,
        in_specs=placed,
        out_specs=P("row", None, "depth", "col"),
        check_vma=False,
    )
```

profile of v0, /device:TPU:5, one launch (start us, length us, event | category | flops | bytes accessed | tf_op | source)
XLA Modules:
  0.0 430.9 jit_solution(2655064788858189192)
XLA Ops:
  0.0 11.8 %copy.50 = bf16[1,18,128,2048]{3,1,2,0:T(8,128)(2,1)S(1)} copy(bf16[1,18,128,2048]{3,2,1,0:T(8,128)(2,1)} %param.14) | data formatting | bytes 18874368 | tf_op args[0]
  11.8 1.3 collective-permute-start
  13.1 3.0 collective-permute-start.1
  16.1 0.0 collective-permute-done
  16.1 0.9 collective-permute-done.1
  17.1 3.0 pad_maximum_fusion.1
  20.0 0.0 copy-start.2
  20.1 4.6 %copy-done.2 = bf16[18,130,2048]{2,0,1:T(8,128)(2,1)} copy-done((bf16[18,130,2048]{2,0,1:T(8,128)(2,1)}, bf16[18,130,2048]{2,0,1:T(8,128)(2,1)S(1)}, u32[]{:S(2)}) %copy-start.2) | copy-done | bytes 9584664
  24.6 0.4 fusion.18
  25.1 0.7 copy.37
  25.7 3.1 collective-permute-start.2
  28.9 0.7 copy.38
  29.5 3.1 collective-permute-start.3
  33.3 11.0 %copy.40 = bf16[18,130,2048]{2,1,0:T(8,128)(2,1)} copy(bf16[18,130,2048]{2,0,1:T(8,128)(2,1)} %copy-done.2) | data formatting | bytes 19169280 | tf_op jit(solution)/shard_map/concatenate | solution.py:19
  44.2 0.0 collective-permute-done.2
  44.3 0.4 copy.39
  44.6 0.0 collective-permute-done.3
  44.6 0.4 copy.41
  45.0 0.0 copy-start.7
  45.0 0.0 copy-start.8
  45.1 19.2 %concatenate.13 = bf16[18,130,2050]{2,1,0:T(8,128)(2,1)} concatenate(bf16[18,130,1]{2,1,0:T(8,128)(2,1)S(1)} %copy.39, bf16[18,130,2048]{2,1,0:T(8,128)(2,1)} %copy.40, bf16[18,130,1]{2,1,0:T(8,128)(2,1)S(1)} %copy.41), dimensions={2} | concatenate | bytes 19188000 | tf_op jit(solution)/shard_map/concatenate | solution.py:19
  64.3 0.0 copy-done.7
  64.3 0.0 copy-done.8
  64.3 2.5 conditional.1
  64.3 2.5 broadcast.64
  66.8 0.0 copy-start.9
  66.8 6.9 %copy.52 = f32[4,128,2048]{2,0,1:T(4,128)} copy(f32[4,128,2048]{2,1,0:T(8,128)} %get-tuple-element.623) | data formatting | bytes 8388608 | tf_op jit(solution)/shard_map/cond | solution.py:100
  73.6 234.6 %all-to-all-start = ((f32[1,4,128,2048]{3,1,0,2:T(4,128)}), f32[1,4,128,2048]{3,1,0,2:T(4,128)}, u32[]{:S(2)}, u32[]{:S(2)}) async-start(f32[1,4,128,2048]{3,1,0,2:T(4,128)} %bitcast.118), calls=%async_computation | async-start | bytes 8388608 | tf_op jit(solution)/shard_map/all_to_all | solution.py:102
  308.3 0.0 copy-done.9
  308.3 94.6 %all-to-all-done = f32[1,4,128,2048]{3,1,0,2:T(4,128)} async-done(((f32[1,4,128,2048]{3,1,0,2:T(4,128)}), f32[1,4,128,2048]{3,1,0,2:T(4,128)}, u32[]{:S(2)}, u32[]{:S(2)}) %all-to-all-start) | async-done | bytes 4194336 | tf_op jit(solution)/shard_map/all_to_all | solution.py:102
  402.9 6.6 %copy.51 = f32[1,4,4,32,2048]{4,3,1,2,0:T(8,128)} copy(f32[1,4,4,32,2048]{4,1,3,2,0:T(4,128)} %bitcast.11) | data formatting | bytes 8388608 | tf_op jit(solution)/shard_map/all_to_all | solution.py:102
  409.5 5.0 %gather_fusion = f32[4,4,32,2048]{3,2,1,0:T(8,128)} fusion(f32[4,4,32,2048]{3,2,1,0:T(8,128)} %bitcast.119, s32[1024]{0:T(1024)S(1)} %pad_clamp_fusion), kind=kCustom, calls=%fused_computation | custom fusion | bytes 8388624 | tf_op jit(solution)/shard_map/jit(_take)/gather | solution.py:74
  414.4 4.9 %broadcast_select_fusion.2 = f32[4,4,32,2048]{3,2,1,0:T(8,128)} fusion(f32[4,4,32,2048]{3,2,1,0:T(8,128)} %gather_fusion, pred[4]{0:T(512)(128)(4,1)S(1)} %compare_and_fusion), kind=kLoop, calls=%fused_computation.39 | loop fusion | flops 1048576 | bytes 8388612 | tf_op jit(solution)/shard_map/jit(_take)/select_n | solution.py:74
  419.3 10.6 %while.28 = (s32[]{:T(128)}, f32[32,2048]{1,0:T(8,128)S(1)}, f32[4,32,2048]{2,1,0:T(8,128)S(1)}, f32[4,4,32,2048]{3,2,1,0:T(8,128)}, s32[]{:T(128)}, /*index=5*/s32[]{:T(128)}, s32[]{}) while((s32[]{:T(128)}, f32[32,2048]{1,0:T(8,128)S(1)}, f32[4,32,2048]{2,1,0:T(8,128)S(1)}, f32[4,4,32,2048]{3,2,1,0:T(8,128)}, s32[]{:T(128)}, ...), condition=%wide.region_9.10_spmd.clone, body=%wide.region_8.9_spmd.clone.sunk | while | flops 983044 | bytes 4456560 | solution.py:85
  419.3 1.0 fusion.26
  420.3 1.6 fusion.27
  422.0 1.0 fusion.26
  423.0 1.6 fusion.27
  424.6 1.0 fusion.26
  425.7 1.6 fusion.27
  427.3 1.0 fusion.26
  428.3 1.6 fusion.27
  430.0 0.0 copy-start.3
  430.0 1.0 copy-done.3
  (6 shorter events, 0.0 us)
Async XLA Ops:
  11.8 4.3 %collective-permute-start = (bf16[18,1,2048]{2,0,1:T(8,128)(2,1)S(1)}, bf16[18,1,2048]{2,0,1:T(8,128)(2,1)S(1)}, u32[]{:S(2)}, u32[]{:S(2)}) collective-permute-start(bf16[18,1,2048]{2,0,1:T(8,128)(2,1)S(1)} %get-tuple-element.371), channel_id=1, source_target_pairs={{0,4},{1,5},{2,6},{3,7},{8,12},{9,13},{10,14},{11,15},{16,20},{17,... | collective-permute-start | bytes 221192 | tf_op jit(solution)/shard_map/ppermute | solution.py:17
  13.1 4.0 collective-permute-start.1
  20.0 4.6 %copy-start.2 = (bf16[18,130,2048]{2,0,1:T(8,128)(2,1)}, bf16[18,130,2048]{2,0,1:T(8,128)(2,1)S(1)}, u32[]{:S(2)}) copy-start(bf16[18,130,2048]{2,0,1:T(8,128)(2,1)S(1)} %pad_maximum_fusion.1) | copy-start | bytes 28753924
  25.7 18.5 %collective-permute-start.2 = (bf16[18,130,1]{1,0,2:T(8,128)(2,1)S(1)}, bf16[18,130,1]{1,0,2:T(8,128)(2,1)S(1)}, u32[]{:S(2)}, u32[]{:S(2)}) collective-permute-start(bf16[18,130,1]{1,0,2:T(8,128)(2,1)S(1)} %copy.37), channel_id=1, source_target_pairs={{0,1},{1,2},{2,3},{4,5},{5,6},{6,7},{8,9},{9,10},{10,11},{12,13},{... | collective-permute-start | bytes 14048 | tf_op jit(solution)/shard_map/ppermute | solution.py:17
  29.5 15.1 %collective-permute-start.3 = (bf16[18,130,1]{1,0,2:T(8,128)(2,1)S(1)}, bf16[18,130,1]{1,0,2:T(8,128)(2,1)S(1)}, u32[]{:S(2)}, u32[]{:S(2)}) collective-permute-start(bf16[18,130,1]{1,0,2:T(8,128)(2,1)S(1)} %copy.38), channel_id=1, source_target_pairs={{1,0},{2,1},{3,2},{5,4},{6,5},{7,6},{9,8},{10,9},{11,10},{13,12},{... | collective-permute-start | bytes 14048 | tf_op jit(solution)/shard_map/ppermute | solution.py:18
  45.0 19.3 %copy-start.7 = (f32[4]{0:T(128)S(1)}, f32[4]{0:T(128)}, u32[]{:S(2)}) copy-start(f32[4]{0:T(128)} %param.18) | copy-start | bytes 52
  45.0 19.2 %copy-start.8 = (f32[3]{0:T(128)S(1)}, f32[3]{0:T(128)}, u32[]{:S(2)}) copy-start(f32[3]{0:T(128)} %param.21) | copy-start | bytes 40
  66.8 241.5 %copy-start.9 = (s32[4]{0:T(128)S(1)}, s32[4]{0:T(128)}, u32[]{:S(2)}) copy-start(s32[4]{0:T(128)} %param.15) | copy-start | bytes 52
  73.6 329.2 %all-to-all-start = ((f32[1,4,128,2048]{3,1,0,2:T(4,128)}), f32[1,4,128,2048]{3,1,0,2:T(4,128)}, u32[]{:S(2)}, u32[]{:S(2)}) async-start(f32[1,4,128,2048]{3,1,0,2:T(4,128)} %bitcast.118), calls=%async_computation | async-start | bytes 8388608 | tf_op jit(solution)/shard_map/all_to_all | solution.py:102
  430.0 1.0 copy-start.3
where the time goes:
time: 438 us; the launch traced here: 431 us
  starting transfers between devices  245 us (56%)
  waiting for transfers between devices  95.5 us (22%)
  local copies, waits for them, and re-layouts  71 us (16%)
  other arithmetic  18.4 us (4%)
    all_to_all x1, starting transfers between devices, per_device(): lax.all_to_all(layer_image[None], 'depth', split_axis=2, concat_axis=0, t...  235 us
    all_to_all x1, waiting for transfers between devices, per_device(): lax.all_to_all(layer_image[None], 'depth', split_axis=2, concat_axis=0, t...  94.6 us
    concatenate x2, local copies, waits for them, and re-layouts, with_halo(): x = jnp.concatenate([before, x, after], axis=dim)  30.2 us
    unnamed x11, local copies, waits for them, and re-layouts  17.3 us
  transfers between devices with their start and end apart: 5, of which 2 were waited for; matrix products, arithmetic and copies ran while one was open for 3% of the time, Pallas kernels for 0%

commit v1 on v0

--- a/solution.py
+++ b/solution.py
@@ -99,7 +99,16 @@
 
     layer_image = lax.cond(empty[0, 0, 0] == 1, blank_layer, lit_layer)
     band_rows = composite(
-        lax.all_to_all(layer_image[None], "depth", split_axis=2, concat_axis=0, tiled=True), order
+        jnp.concatenate(
+            lax.all_to_all(
+                jnp.stack(jnp.split(layer_image[None], lax.axis_size("depth"), axis=2)),
+                "depth",
+                0,
+                0,
+            ),
+            axis=0,
+        ),
+        order,
     )
     return band_rows[None]
 

time: 438 us -> 404 us (0.922); the launches traced: 431 us -> 402 us
  local copies, waits for them, and re-layouts: 71 us -> 55.4 us
  starting transfers between devices: 245 us -> 230 us
    all_to_all x1, starting transfers between devices: 235 us -> 219 us  [per_device(): lax.all_to_all(jnp.stack(jnp.split(layer_image[None], lax.axis_size('dept...]
    cond x1 -> x0, local copies, waits for them, and re-layouts: 6.87 us -> none  [per_device(): layer_image = lax.cond(empty[0, 0, 0] == 1, blank_layer, lit_layer)]
    all_to_all x1 -> x0, local copies, waits for them, and re-layouts: 6.59 us -> none  [per_device(): lax.all_to_all(layer_image[None], 'depth', split_axis=2, concat_axis=0, t...]
where the time goes in v1:
time: 404 us; the launch traced here: 402 us
  starting transfers between devices  230 us (57%)
  waiting for transfers between devices  95.5 us (24%)
  local copies, waits for them, and re-layouts  55.4 us (14%)
  other arithmetic  20.7 us (5%)
    all_to_all x1, starting transfers between devices, per_device(): lax.all_to_all(jnp.stack(jnp.split(layer_image[None], lax.axis_size('dept...  219 us
    all_to_all x1, waiting for transfers between devices, per_device(): lax.all_to_all(jnp.stack(jnp.split(layer_image[None], lax.axis_size('dept...  94.6 us
    concatenate x2, local copies, waits for them, and re-layouts, with_halo(): x = jnp.concatenate([before, x, after], axis=dim)  30.2 us
    unnamed x11, local copies, waits for them, and re-layouts  17.3 us
  transfers between devices with their start and end apart: 5, of which 2 were waited for; matrix products, arithmetic and copies ran while one was open for 3% of the time, Pallas kernels for 0%

profile of v1, /device:TPU:5, one launch (start us, length us, event | category | flops | bytes accessed | tf_op | source)
XLA Modules:
  0.0 402.3 jit_solution(17716807078425363423)
XLA Ops:
  0.0 11.8 %copy.31 = bf16[1,18,128,2048]{3,1,2,0:T(8,128)(2,1)S(1)} copy(bf16[1,18,128,2048]{3,2,1,0:T(8,128)(2,1)} %param.14) | data formatting | bytes 18874368 | tf_op args[0]
  11.8 1.3 collective-permute-start
  13.1 3.0 collective-permute-start.1
  16.1 0.0 collective-permute-done
  16.1 0.9 collective-permute-done.1
  17.1 3.0 pad_maximum_fusion
  20.0 0.0 copy-start.2
  20.1 4.6 %copy-done.2 = bf16[18,130,2048]{2,0,1:T(8,128)(2,1)} copy-done((bf16[18,130,2048]{2,0,1:T(8,128)(2,1)}, bf16[18,130,2048]{2,0,1:T(8,128)(2,1)S(1)}, u32[]{:S(2)}) %copy-start.2) | copy-done | bytes 9584664
  24.6 0.4 fusion.18
  25.1 0.7 copy.25
  25.7 3.1 collective-permute-start.2
  28.9 0.7 copy.26
  29.5 3.1 collective-permute-start.3
  33.3 10.9 %copy.28 = bf16[18,130,2048]{2,1,0:T(8,128)(2,1)} copy(bf16[18,130,2048]{2,0,1:T(8,128)(2,1)} %copy-done.2) | data formatting | bytes 19169280 | tf_op jit(solution)/shard_map/concatenate | solution.py:19
  44.2 0.0 collective-permute-done.2
  44.2 0.4 copy.27
  44.6 0.0 collective-permute-done.3
  44.6 0.4 copy.29
  45.0 0.0 copy-start.7
  45.0 0.0 copy-start.8
  45.0 19.2 %concatenate.14 = bf16[18,130,2050]{2,1,0:T(8,128)(2,1)} concatenate(bf16[18,130,1]{2,1,0:T(8,128)(2,1)S(1)} %copy.27, bf16[18,130,2048]{2,1,0:T(8,128)(2,1)} %copy.28, bf16[18,130,1]{2,1,0:T(8,128)(2,1)S(1)} %copy.29), dimensions={2} | concatenate | bytes 19188000 | tf_op jit(solution)/shard_map/concatenate | solution.py:19
  64.2 0.0 copy-done.7
  64.2 0.0 copy-done.8
  64.2 0.4 conditional.1
  64.2 0.1 stack.51
  64.3 0.1 stack.51.clone
  64.4 0.1 stack.51.clone.1
  64.5 0.1 stack.51.clone.2
  64.6 0.0 copy-start.9
  64.6 2.3 pad_maximum_fusion.1
  66.9 219.3 %all-to-all-start = ((f32[4,1,4,32,2048]{4,3,2,1,0:T(8,128)}), f32[4,1,4,32,2048]{4,3,2,1,0:T(8,128)}, u32[]{:S(2)}, u32[]{:S(2)}) async-start(f32[4,1,4,32,2048]{4,3,2,1,0:T(8,128)} %pad_maximum_fusion.1), calls=%async_computation | async-start | bytes 8388608 | tf_op jit(solution)/shard_map/all_to_all | solution.py:103
  286.2 0.0 copy-done.9
  286.2 94.6 %all-to-all-done = f32[4,1,4,32,2048]{4,3,2,1,0:T(8,128)} async-done(((f32[4,1,4,32,2048]{4,3,2,1,0:T(8,128)}), f32[4,1,4,32,2048]{4,3,2,1,0:T(8,128)}, u32[]{:S(2)}, u32[]{:S(2)}) %all-to-all-start) | async-done | bytes 4194336 | tf_op jit(solution)/shard_map/all_to_all | solution.py:103
  380.8 5.0 %gather_fusion = f32[4,4,32,2048]{3,2,1,0:T(8,128)} fusion(f32[4,4,32,2048]{3,2,1,0:T(8,128)} %bitcast.15, s32[1024]{0:T(1024)S(1)} %pad_clamp_fusion), kind=kCustom, calls=%fused_computation | custom fusion | bytes 8388624 | tf_op jit(solution)/shard_map/jit(_take)/gather | solution.py:74
  385.8 4.9 %broadcast_select_fusion.2 = f32[4,4,32,2048]{3,2,1,0:T(8,128)} fusion(f32[4,4,32,2048]{3,2,1,0:T(8,128)} %gather_fusion, pred[4]{0:T(512)(128)(4,1)S(1)} %compare_and_fusion), kind=kLoop, calls=%fused_computation.42 | loop fusion | flops 1048576 | bytes 8388612 | tf_op jit(solution)/shard_map/jit(_take)/select_n | solution.py:74
  390.7 10.6 %while.31 = (s32[]{:T(128)}, f32[32,2048]{1,0:T(8,128)S(1)}, f32[4,32,2048]{2,1,0:T(8,128)S(1)}, f32[4,4,32,2048]{3,2,1,0:T(8,128)}, s32[]{:T(128)}, /*index=5*/s32[]{:T(128)}, s32[]{}) while((s32[]{:T(128)}, f32[32,2048]{1,0:T(8,128)S(1)}, f32[4,32,2048]{2,1,0:T(8,128)S(1)}, f32[4,4,32,2048]{3,2,1,0:T(8,128)}, s32[]{:T(128)}, ...), condition=%wide.region_9.10_spmd.clone, body=%wide.region_8.9_spmd.clone.sunk | while | flops 983044 | bytes 4456560 | solution.py:85
  390.7 1.0 fusion.26
  391.7 1.6 fusion.27
  393.3 1.0 fusion.26
  394.4 1.6 fusion.27
  396.0 1.0 fusion.26
  397.0 1.6 fusion.27
  398.7 1.0 fusion.26
  399.7 1.6 fusion.27
  401.3 0.0 copy-start.3
  401.3 1.0 copy-done.3
  (6 shorter events, 0.0 us)
Async XLA Ops:
  11.8 4.3 %collective-permute-start = (bf16[18,1,2048]{2,0,1:T(8,128)(2,1)S(1)}, bf16[18,1,2048]{2,0,1:T(8,128)(2,1)S(1)}, u32[]{:S(2)}, u32[]{:S(2)}) collective-permute-start(bf16[18,1,2048]{2,0,1:T(8,128)(2,1)S(1)} %get-tuple-element.392), channel_id=1, source_target_pairs={{0,4},{1,5},{2,6},{3,7},{8,12},{9,13},{10,14},{11,15},{16,20},{17,... | collective-permute-start | bytes 221192 | tf_op jit(solution)/shard_map/ppermute | solution.py:17
  13.1 4.0 collective-permute-start.1
  20.0 4.6 %copy-start.2 = (bf16[18,130,2048]{2,0,1:T(8,128)(2,1)}, bf16[18,130,2048]{2,0,1:T(8,128)(2,1)S(1)}, u32[]{:S(2)}) copy-start(bf16[18,130,2048]{2,0,1:T(8,128)(2,1)S(1)} %pad_maximum_fusion) | copy-start | bytes 28753924
  25.7 18.5 %collective-permute-start.2 = (bf16[18,130,1]{1,0,2:T(8,128)(2,1)S(1)}, bf16[18,130,1]{1,0,2:T(8,128)(2,1)S(1)}, u32[]{:S(2)}, u32[]{:S(2)}) collective-permute-start(bf16[18,130,1]{1,0,2:T(8,128)(2,1)S(1)} %copy.25), channel_id=1, source_target_pairs={{0,1},{1,2},{2,3},{4,5},{5,6},{6,7},{8,9},{9,10},{10,11},{12,13},{... | collective-permute-start | bytes 14048 | tf_op jit(solution)/shard_map/ppermute | solution.py:17
  29.5 15.1 %collective-permute-start.3 = (bf16[18,130,1]{1,0,2:T(8,128)(2,1)S(1)}, bf16[18,130,1]{1,0,2:T(8,128)(2,1)S(1)}, u32[]{:S(2)}, u32[]{:S(2)}) collective-permute-start(bf16[18,130,1]{1,0,2:T(8,128)(2,1)S(1)} %copy.26), channel_id=1, source_target_pairs={{1,0},{2,1},{3,2},{5,4},{6,5},{7,6},{9,8},{10,9},{11,10},{13,12},{... | collective-permute-start | bytes 14048 | tf_op jit(solution)/shard_map/ppermute | solution.py:18
  45.0 19.2 %copy-start.7 = (f32[4]{0:T(128)S(1)}, f32[4]{0:T(128)}, u32[]{:S(2)}) copy-start(f32[4]{0:T(128)} %param.18) | copy-start | bytes 52
  45.0 19.2 %copy-start.8 = (f32[3]{0:T(128)S(1)}, f32[3]{0:T(128)}, u32[]{:S(2)}) copy-start(f32[3]{0:T(128)} %param.21) | copy-start | bytes 40
  64.6 221.5 %copy-start.9 = (s32[4]{0:T(128)S(1)}, s32[4]{0:T(128)}, u32[]{:S(2)}) copy-start(s32[4]{0:T(128)} %param.15) | copy-start | bytes 52
  66.9 313.9 %all-to-all-start = ((f32[4,1,4,32,2048]{4,3,2,1,0:T(8,128)}), f32[4,1,4,32,2048]{4,3,2,1,0:T(8,128)}, u32[]{:S(2)}, u32[]{:S(2)}) async-start(f32[4,1,4,32,2048]{4,3,2,1,0:T(8,128)} %pad_maximum_fusion.1), calls=%async_computation | async-start | bytes 8388608 | tf_op jit(solution)/shard_map/all_to_all | solution.py:103
  401.3 1.0 copy-start.3
